TPU v7x, 32 devices: a whole 2x2x4 slice. The times are simulated.
32 devices in a mesh: dp: 4 (over y, x), seq: 4 (over z), tp: 2 (over core).
Axes of the slice: x: 2, y: 2, z: 4, core: 2. Of those that a mesh axis runs over, the one named last changes fastest.
Arguments:
- queries: bfloat16 [4, 2048, 5120], P('dp', 'seq', 'tp'), may hold values from -200 to 200
- keys: bfloat16 [4, 512, 5120], P('dp', None, 'tp'), may hold values from -6 to 6
- values: bfloat16 [4, 512, 5120], P('dp', None, 'tp'), may hold values from -6 to 6
- grad_attention: bfloat16 [4, 2048, 5120], P('dp', 'seq', 'tp'), may hold values from -48 to 48
- normed: bfloat16 [4, 512, 4096], P('dp', None, 'seq'), may hold values from -6 to 6
- norm_scale: float32 [4, 512], P('dp'), may hold values from 0.3 to 3
- norm_gain: float32 [4096], P('seq'), may hold values from 0.1 to 1.9
- key_weight: bfloat16 [4096, 5120], P('seq', 'tp'), may hold values from -0.078125 to 0.078125
- value_weight: bfloat16 [4096, 5120], P('seq', 'tp'), may hold values from -0.078125 to 0.078125
- key_down: bfloat16 [4096, 32], P('seq'), may hold values from -0.09375 to 0.09375
- key_up: bfloat16 [32, 5120], P(None, 'tp'), may hold values from -0.078125 to 0.078125
- value_down: bfloat16 [4096, 32], P('seq'), may hold values from -0.09375 to 0.09375
- value_up: bfloat16 [32, 5120], P(None, 'tp'), may hold values from -0.078125 to 0.078125
- out_weight: bfloat16 [10240, 4096], P('tp', 'seq'), may hold values from -0.09375 to 0.09375
Outputs:
- grad_queries: bfloat16 [4, 2048, 5120], P('dp', 'seq', 'tp')
- grad_text: bfloat16 [4, 512, 4096], P('dp', None, 'seq')
- grad_hidden: bfloat16 [4, 512, 10240], P('dp', 'seq', 'tp')
- grad_key_down: float32 [4096, 32], P('seq')
- grad_key_up: float32 [32, 5120], P(None, 'tp')
- grad_value_down: float32 [4096, 32], P('seq')
- grad_value_up: float32 [32, 5120], P(None, 'tp')
All inputs are finite; a program needn't handle non-finite values.
Results may differ from a plain program's by a relative error of at most 0.03.
Values may be sent and summed in bfloat16 or wider, within the bound.
A program may use at most 192 MiB of HBM per device.

v0:
```python
import functools

import jax
import jax.numpy as jnp
from jax import lax
from jax.experimental import pallas as pl
from jax.experimental.pallas import tpu as pltpu
from jax.sharding import PartitionSpec as P

HD = 128
MESH = pl.DeviceIdType.MESH


def dot(left_side, right_side, left_dim, right_dim):
    return lax.dot_general(
        left_side,
        right_side,
        (((left_dim,), (right_dim,)), ((), ())),
        preferred_element_type=jnp.float32,
    )


def attention_kernel(
    n,
    heads,
    lag,
    queries,
    keys,
    values,
    grads,
    key_weight,
    value_weight,
    key_up,
    value_up,
    grad_query,
    key_grad,
    value_grad,
    context,
    project,
    part,
    up_in,
    up_out,
    down_in,
    down_out,
    total,
    key_total,
    value_total,
    up_send,
    up_recv,
    down_send,
    down_recv,
):
    step = pl.program_id(0)
    me = lax.axis_index("seq")
    factor = HD ** (-0.5)
    has_low = me > 0
    has_high = me < n - 1

    def up_copy(chunk, half, source):
        return pltpu.make_async_remote_copy(
            src_ref=source.at[chunk, half],
            dst_ref=up_in.at[chunk, half],
            send_sem=up_send.at[chunk, half],
            recv_sem=up_recv.at[chunk, half],
            device_id={"seq": lax.rem(me + 1, n)},
            device_id_type=MESH,
        )

    def down_copy(chunk, half, source):
        return pltpu.make_async_remote_copy(
            src_ref=source.at[chunk, half],
            dst_ref=down_in.at[chunk, half],
            send_sem=down_send.at[chunk, half],
            recv_sem=down_recv.at[chunk, half],
            device_id={"seq": lax.rem(me + n - 1, n)},
            device_id_type=MESH,
        )

    @pl.when(step == 0)
    def _():
        barrier = pltpu.get_barrier_semaphore()

        @pl.when(has_low)
        def _():
            pl.semaphore_signal(
                barrier,
                inc=1,
                device_id={"seq": lax.rem(me + n - 1, n)},
                device_id_type=MESH,
            )

        @pl.when(has_high)
        def _():
            pl.semaphore_signal(
                barrier, inc=1, device_id={"seq": lax.rem(me + 1, n)}, device_id_type=MESH
            )

        total[...] = jnp.zeros_like(total)
        key_total[...] = jnp.zeros_like(key_total)
        value_total[...] = jnp.zeros_like(value_total)

        pl.semaphore_wait(barrier, has_low.astype(jnp.int32) + has_high.astype(jnp.int32))

    @pl.when(step < heads)
    def _():
        query, key, value, grad = queries[...], keys[...], values[...], grads[...]
        scores = dot(key, query, 1, 1) * factor
        weights = jnp.exp(scores - jnp.max(scores, axis=0, keepdims=True))
        probability = weights * (1.0 / jnp.sum(weights, axis=0, keepdims=True))
        part[step, 1] = dot(probability.astype(jnp.bfloat16), grad, 1, 0).astype(jnp.bfloat16)
        grad_probs = dot(value, grad, 1, 1)
        grad_scores = probability * (
            grad_probs - jnp.sum(probability * grad_probs, axis=0, keepdims=True)
        )
        grad_low = grad_scores.astype(jnp.bfloat16)
        part[step, 0] = (dot(grad_low, query, 1, 0) * factor).astype(jnp.bfloat16)
        grad_query[...] = (dot(grad_low, key, 0, 0) * factor).astype(jnp.bfloat16)

    up_chunk = step - me
    up_live = jnp.logical_and(up_chunk >= 0, up_chunk < heads)
    down_chunk = step - (n - 1 - me)
    down_live = jnp.logical_and(down_chunk >= 0, down_chunk < heads)

    @pl.when(jnp.logical_and(up_live, me == 0))
    def _():
        for half in (1, 0):
            up_copy(up_chunk, half, part).start()
        up_in[up_chunk] = jnp.zeros(up_in.shape[1:], up_in.dtype)

    @pl.when(jnp.logical_and(down_live, me == n - 1))
    def _():
        for half in (1, 0):
            down_copy(down_chunk, half, part).start()
        down_in[down_chunk] = jnp.zeros(down_in.shape[1:], down_in.dtype)

    for half in (1, 0):

        @pl.when(jnp.logical_and(up_live, has_low))
        def _():
            up_copy(up_chunk, half, up_out).wait_recv()

            @pl.when(has_high)
            def _():
                up_out[up_chunk, half] = up_in[up_chunk, half] + part[up_chunk, half]
                up_copy(up_chunk, half, up_out).start()

        @pl.when(jnp.logical_and(down_live, has_high))
        def _():
            down_copy(down_chunk, half, down_out).wait_recv()

            @pl.when(has_low)
            def _():
                down_out[down_chunk, half] = down_in[down_chunk, half] + part[down_chunk, half]
                down_copy(down_chunk, half, down_out).start()

    @pl.when(step >= lag)
    def _():
        chunk = step - lag

        @pl.when(has_high)
        def _():
            for half in (1, 0):
                up_copy(chunk, half, up_out).wait_send()

        @pl.when(has_low)
        def _():
            for half in (1, 0):
                down_copy(chunk, half, down_out).wait_send()

        both = (
            up_in[chunk].astype(jnp.float32)
            + part[chunk].astype(jnp.float32)
            + down_in[chunk].astype(jnp.float32)
        ).astype(jnp.bfloat16)
        key_grad[...] = both[0]
        value_grad[...] = both[1]
        slab = jnp.concatenate([key_weight[...], value_weight[...]], axis=1)
        total[...] += dot(jnp.concatenate([both[0], both[1]], axis=1), slab, 1, 1)
        key_total[...] += dot(both[0], key_up[...], 1, 1)
        value_total[...] += dot(both[1], value_up[...], 1, 1)

    @pl.when(step == heads + lag - 1)
    def _():
        context[...] = total[...].astype(jnp.bfloat16)
        project[...] = jnp.concatenate([key_total[...], value_total[...]], axis=1).astype(
            jnp.bfloat16
        )


def attention_grads(
    queries, keys, values, grad_attention, key_weight, value_weight, key_up, value_up
):
    rows, columns = queries.shape
    length = keys.shape[0]
    features = key_weight.shape[0]
    rank = key_up.shape[0]
    heads = columns // HD
    n = lax.axis_size("seq")
    lag = n + 1

    def early(height):
        return pl.BlockSpec((height, HD), lambda step: (0, jnp.minimum(step, heads - 1)))

    def late(height):
        return pl.BlockSpec((height, HD), lambda step: (0, jnp.maximum(step - lag, 0)))

    def fixed(height, width):
        return pl.BlockSpec((height, width), lambda step: (0, 0))

    buffer = pltpu.VMEM((heads, 2, length, HD), jnp.bfloat16)
    semaphores = pltpu.SemaphoreType.DMA((heads, 2))
    return pl.pallas_call(
        functools.partial(attention_kernel, n, heads, lag),
        grid=(heads + lag,),
        out_shape=(
            jax.ShapeDtypeStruct((rows, columns), jnp.bfloat16),
            jax.ShapeDtypeStruct((length, columns), jnp.bfloat16),
            jax.ShapeDtypeStruct((length, columns), jnp.bfloat16),
            jax.ShapeDtypeStruct((length, features), jnp.bfloat16),
            jax.ShapeDtypeStruct((length, 2 * rank), jnp.bfloat16),
        ),
        in_specs=[
            early(rows),
            early(length),
            early(length),
            early(rows),
            late(features),
            late(features),
            late(rank),
            late(rank),
        ],
        out_specs=(
            early(rows),
            late(length),
            late(length),
            fixed(length, features),
            fixed(length, 2 * rank),
        ),
        scratch_shapes=[buffer] * 5
        + [
            pltpu.VMEM((length, features), jnp.float32),
            pltpu.VMEM((length, rank), jnp.float32),
            pltpu.VMEM((length, rank), jnp.float32),
        ]
        + [semaphores] * 4,
        compiler_params=pltpu.CompilerParams(
            collective_id=0, has_side_effects=True, vmem_limit_bytes=50 * 1024 * 1024
        ),
        cost_estimate=pl.CostEstimate(
            flops=14 * rows * length * columns,
            bytes_accessed=12 * rows * columns,
            transcendentals=rows * length * heads,
        ),
        name="attention",
    )(queries, keys, values, grad_attention, key_weight, value_weight, key_up, value_up)


def exchange(axis, size, source, landing, send, recv):
    me = lax.axis_index(axis)

    def copy(offset):
        return pltpu.make_async_remote_copy(
            src_ref=source,
            dst_ref=landing.at[me],
            send_sem=send.at[offset],
            recv_sem=recv.at[me],
            device_id={axis: lax.rem(me + offset, size)},
            device_id_type=MESH,
        )

    def arrival(offset):
        other = lax.rem(me + offset, size)
        return pltpu.make_async_remote_copy(
            src_ref=source,
            dst_ref=landing.at[other],
            send_sem=send.at[offset],
            recv_sem=recv.at[other],
            device_id={axis: other},
            device_id_type=MESH,
        )

    def start():
        for offset in range(1, size):
            copy(offset).start()

    def finish():
        for offset in range(1, size):
            arrival(offset).wait_recv()
        for offset in range(1, size):
            copy(offset).wait_send()

    return start, finish


def tail_kernel(
    n,
    splits,
    prompts,
    slices,
    features_whole,
    context_part,
    project_part,
    normed,
    scale,
    gain,
    key_down,
    value_down,
    key_grad,
    value_grad,
    out_weight,
    grad_text,
    grad_hidden,
    key_down_grad,
    value_down_grad,
    key_up_grad,
    value_up_grad,
    weight,
    grads,
    context_all,
    project_all,
    scaled,
    sum_own,
    sum_all,
    up_own,
    up_all,
    down_own,
    down_all,
    rows_own,
    rows_all,
    latent_own,
    latent_all,
    part,
    up_in,
    up_out,
    down_in,
    down_out,
    weight_sem,
    grads_sem,
    context_send,
    context_recv,
    project_send,
    project_recv,
    sum_send,
    sum_recv,
    up_dp_send,
    up_dp_recv,
    down_dp_send,
    down_dp_recv,
    rows_send,
    rows_recv,
    latent_send,
    latent_recv,
    high_send,
    high_recv,
    low_send,
    low_recv,
):
    me = lax.axis_index("seq")
    split = lax.axis_index("tp")
    prompt = lax.axis_index("dp")
    length = grad_text.shape[0]
    width = part.shape[3]
    block = part.shape[2]
    lag = n
    has_low = me > 0
    has_high = me < n - 1

    key_fetch = pltpu.make_async_copy(key_grad, grads, grads_sem)
    value_fetch = pltpu.make_async_copy(value_grad, grads, grads_sem)
    weight_fetch = pltpu.make_async_copy(out_weight, weight, weight_sem)

    @pl.when(me < n // 2)
    def _():
        key_fetch.start()

    @pl.when(me >= n // 2)
    def _():
        value_fetch.start()

    weight_fetch.start()

    barrier = pltpu.get_barrier_semaphore()
    for axis, size in (("tp", splits), ("seq", n), ("dp", prompts)):
        for offset in range(1, size):
            pl.semaphore_signal(
                barrier,
                inc=1,
                device_id={axis: lax.rem(lax.axis_index(axis) + offset, size)},
                device_id_type=MESH,
            )
    pl.semaphore_wait(barrier, splits + n + prompts - 3)

    project_start, project_finish = exchange(
        "tp", splits, project_part, project_all, project_send, project_recv
    )
    context_start, context_finish = exchange(
        "tp", splits, context_part, context_all, context_send, context_recv
    )
    sum_start, sum_finish = exchange("seq", n, sum_own, sum_all, sum_send, sum_recv)
    up_start, up_finish = exchange("dp", prompts, up_own, up_all, up_dp_send, up_dp_recv)
    down_start, down_finish = exchange(
        "dp", prompts, down_own, down_all, down_dp_send, down_dp_recv
    )
    rows_start, rows_finish = exchange("seq", n, rows_own, rows_all, rows_send, rows_recv)

    def latent_copy(offset):
        other = lax.rem(me + offset, n)
        return pltpu.make_async_remote_copy(
            src_ref=latent_own.at[other],
            dst_ref=latent_all.at[me],
            send_sem=latent_send.at[offset],
            recv_sem=latent_recv.at[me],
            device_id={"seq": other},
            device_id_type=MESH,
        )

    def latent_arrival(offset):
        other = lax.rem(me + offset, n)
        return pltpu.make_async_remote_copy(
            src_ref=latent_own.at[other],
            dst_ref=latent_all.at[other],
            send_sem=latent_send.at[offset],
            recv_sem=latent_recv.at[other],
            device_id={"seq": other},
            device_id_type=MESH,
        )

    project_start()
    context_start()
    project_all[split] = project_part[...]
    context_all[split] = context_part[...]
    context = (normed[...].astype(jnp.float32) * gain[...]).astype(jnp.bfloat16)
    latent_rows = jnp.concatenate(
        [dot(key_down[...], context, 1, 1), dot(value_down[...], context, 1, 1)], axis=0
    )
    latent_own[...] = latent_rows.reshape(latent_own.shape).astype(jnp.bfloat16)
    for offset in range(1, n):
        latent_copy(offset).start()
    latent_all[me] = latent_own[me]

    project_finish()
    back = project_all[0].astype(jnp.float32)
    for index in range(1, splits):
        back = back + project_all[index].astype(jnp.float32)
    back = back.astype(jnp.bfloat16)
    rank = key_down.shape[0]
    low_rank = dot(back[:, :rank], key_down[...], 1, 0) + dot(
        back[:, rank:], value_down[...], 1, 0
    )
    context_finish()
    whole = context_all[0].astype(jnp.float32)
    for index in range(1, splits):
        whole = whole + context_all[index].astype(jnp.float32)
    scaled[...] = gain[...] * (whole + low_rank)
    local_sum = jnp.sum(normed[...].astype(jnp.float32) * scaled[...], axis=1, keepdims=True)
    sum_own[...] = jnp.transpose(jnp.broadcast_to(local_sum, (length, 128)))[:8, :]
    sum_all[me] = sum_own[...]
    sum_start()

    down_own[...] = dot(back, context, 0, 0).astype(jnp.bfloat16)
    down_all[prompt] = down_own[...]
    down_start()
    for offset in range(1, n):
        latent_arrival(offset).wait_recv()
    latent = latent_all[0].astype(jnp.float32)
    for index in range(1, n):
        latent = latent + latent_all[index].astype(jnp.float32)
    key_fetch.wait()
    up_own[...] = dot(latent.astype(jnp.bfloat16), grads[...], 1, 0).astype(jnp.bfloat16)
    up_all[prompt] = up_own[...]
    up_start()
    weight_fetch.wait()
    for offset in range(1, n):
        latent_copy(offset).wait_send()

    sum_finish()
    token_sum = sum_all[0]
    for index in range(1, n):
        token_sum = token_sum + sum_all[index]
    token_column = jnp.transpose(jnp.broadcast_to(token_sum[:1, :], (128, length)))[:, :1]
    grad_text[...] = (
        scale[...]
        * (scaled[...] - normed[...].astype(jnp.float32) * (token_column / features_whole))
    ).astype(jnp.bfloat16)

    def high_copy(chunk, owner, source):
        return pltpu.make_async_remote_copy(
            src_ref=source.at[chunk, owner],
            dst_ref=up_in.at[chunk, owner],
            send_sem=high_send.at[chunk, owner],
            recv_sem=high_recv.at[chunk, owner],
            device_id={"seq": lax.rem(me + 1, n)},
            device_id_type=MESH,
        )

    def low_copy(chunk, owner, source):
        return pltpu.make_async_remote_copy(
            src_ref=source.at[chunk, owner],
            dst_ref=down_in.at[chunk, owner],
            send_sem=low_send.at[chunk, owner],
            recv_sem=low_recv.at[chunk, owner],
            device_id={"seq": lax.rem(me + n - 1, n)},
            device_id_type=MESH,
        )

    def hidden_step(step, carry):
        @pl.when(step < slices)
        def _():
            slab = weight[pl.ds(pl.multiple_of(step * width, width), width), :]
            product = dot(grad_text[...], slab, 1, 1).astype(jnp.bfloat16)
            part[step] = product.reshape(n, block, width)

        high = step - me
        high_live = jnp.logical_and(high >= 0, high < slices)

        @pl.when(jnp.logical_and(high_live, me == 0))
        def _():
            def send(index, carry):
                high_copy(high, n - 1 - index, part).start()
                return carry

            lax.fori_loop(0, n - 1, send, 0)
            up_in[high, 0] = jnp.zeros(up_in.shape[2:], up_in.dtype)

        @pl.when(jnp.logical_and(high_live, has_low))
        def _():
            def forward(index, carry):
                owner = n - 1 - index
                high_copy(high, owner, up_out).wait_recv()
                up_out[high, owner] = up_in[high, owner] + part[high, owner]
                high_copy(high, owner, up_out).start()
                return carry

            lax.fori_loop(0, n - 1 - me, forward, 0)
            high_copy(high, me, up_out).wait_recv()

        low = step - (n - 1 - me)
        low_live = jnp.logical_and(low >= 0, low < slices)

        @pl.when(jnp.logical_and(low_live, me == n - 1))
        def _():
            def send(owner, carry):
                low_copy(low, owner, part).start()
                return carry

            lax.fori_loop(0, n - 1, send, 0)
            down_in[low, n - 1] = jnp.zeros(down_in.shape[2:], down_in.dtype)

        @pl.when(jnp.logical_and(low_live, has_high))
        def _():
            def forward(owner, carry):
                low_copy(low, owner, down_out).wait_recv()
                down_out[low, owner] = down_in[low, owner] + part[low, owner]
                low_copy(low, owner, down_out).start()
                return carry

            lax.fori_loop(0, me, forward, 0)
            low_copy(low, me, down_out).wait_recv()

        @pl.when(step >= lag)
        def _():
            chunk = step - lag

            def high_done(owner, carry):
                high_copy(chunk, owner, up_out).wait_send()
                return carry

            def low_done(owner, carry):
                low_copy(chunk, owner, down_out).wait_send()
                return carry

            lax.fori_loop(me + 1, n, high_done, 0)
            lax.fori_loop(0, me, low_done, 0)
            grad_hidden[:, pl.ds(pl.multiple_of(chunk * width, width), width)] = (
                up_in[chunk, me].astype(jnp.float32)
                + part[chunk, me].astype(jnp.float32)
                + down_in[chunk, me].astype(jnp.float32)
            ).astype(jnp.bfloat16)

        return carry

    lax.fori_loop(0, slices // 2, hidden_step, 0)

    up_finish()
    up_total = up_all[0].astype(jnp.float32)
    for index in range(1, prompts):
        up_total = up_total + up_all[index].astype(jnp.float32)
    rows_own[...] = (up_total / prompts).astype(jnp.bfloat16)
    rows_all[me] = rows_own[...]
    rows_start()
    down_finish()
    down_total = down_all[0].astype(jnp.float32)
    for index in range(1, prompts):
        down_total = down_total + down_all[index].astype(jnp.float32)
    key_down_grad[...] = down_total[:rank] / prompts
    value_down_grad[...] = down_total[rank:] / prompts

    lax.fori_loop(slices // 2, slices + lag, hidden_step, 0)
    rows_finish()
    key_up_grad[...] = rows_all[: n // 2].astype(jnp.float32).reshape(key_up_grad.shape)
    value_up_grad[...] = rows_all[n // 2 :].astype(jnp.float32).reshape(value_up_grad.shape)


def tail(
    context_part,
    project_part,
    normed,
    scale,
    gain,
    key_down,
    value_down,
    key_grad,
    value_grad,
    out_weight,
):
    length, features = context_part.shape
    pair = project_part.shape[1]
    columns = key_grad.shape[1]
    hidden = out_weight.shape[0]
    n, splits, prompts = lax.axis_size("seq"), lax.axis_size("tp"), lax.axis_size("dp")
    width = 512 if hidden % 512 == 0 else 256
    slices = hidden // width
    block = length // n
    share = pair // n
    low = jnp.bfloat16
    buffer = pltpu.VMEM((slices, n, block, width), low)
    dma = pltpu.SemaphoreType.DMA
    vmem = pl.BlockSpec(memory_space=pltpu.VMEM)
    hbm = pl.BlockSpec(memory_space=pl.ANY)
    return pl.pallas_call(
        functools.partial(tail_kernel, n, splits, prompts, slices, features * n),
        out_shape=(
            jax.ShapeDtypeStruct((length, features), low),
            jax.ShapeDtypeStruct((block, hidden), low),
            jax.ShapeDtypeStruct((pair // 2, features), jnp.float32),
            jax.ShapeDtypeStruct((pair // 2, features), jnp.float32),
            jax.ShapeDtypeStruct((pair // 2, columns), jnp.float32),
            jax.ShapeDtypeStruct((pair // 2, columns), jnp.float32),
        ),
        in_specs=[vmem] * 7 + [hbm] * 3,
        out_specs=(vmem,) * 6,
        scratch_shapes=[
            pltpu.VMEM(out_weight.shape, low),
            pltpu.VMEM(key_grad.shape, low),
            pltpu.VMEM((splits, length, features), low),
            pltpu.VMEM((splits, length, pair), low),
            pltpu.VMEM((length, features), jnp.float32),
            pltpu.VMEM((8, length), jnp.float32),
            pltpu.VMEM((n, 8, length), jnp.float32),
            pltpu.VMEM((share, columns), low),
            pltpu.VMEM((prompts, share, columns), low),
            pltpu.VMEM((pair, features), low),
            pltpu.VMEM((prompts, pair, features), low),
            pltpu.VMEM((share, columns), low),
            pltpu.VMEM((n, share, columns), low),
            pltpu.VMEM((n, share, length), low),
            pltpu.VMEM((n, share, length), low),
        ]
        + [buffer] * 5
        + [dma, dma]
        + [dma((splits,))] * 4
        + [dma((n,))] * 2
        + [dma((prompts,))] * 4
        + [dma((n,))] * 4
        + [dma((slices, n))] * 4,
        compiler_params=pltpu.CompilerParams(
            collective_id=1, has_side_effects=True, vmem_limit_bytes=60 * 1024 * 1024
        ),
        name="tail",
    )(
        context_part,
        project_part,
        normed,
        scale,
        gain,
        key_down,
        value_down,
        key_grad,
        value_grad,
        out_weight,
    )


def shards(
    queries,
    keys,
    values,
    grad_attention,
    normed,
    norm_scale,
    norm_gain,
    key_weight,
    value_weight,
    key_down,
    key_up,
    value_down,
    value_up,
    out_weight,
):
    grad_query, key_grad, value_grad, context_part, project_part = attention_grads(
        queries[0],
        keys[0],
        values[0],
        grad_attention[0],
        key_weight,
        value_weight,
        key_up,
        value_up,
    )
    grad_text, grad_hidden, down_key, down_value, up_key, up_value = tail(
        context_part,
        project_part,
        normed[0],
        norm_scale[0][:, None],
        norm_gain[None, :],
        key_down.T,
        value_down.T,
        key_grad,
        value_grad,
        out_weight,
    )
    return (
        grad_query[None],
        grad_text[None],
        grad_hidden[None],
        down_key.T,
        up_key,
        down_value.T,
        up_value,
    )


def solution(mesh):
    return jax.shard_map(
        shards,
        mesh=mesh,
        in_specs=(
            P("dp", "seq", "tp"),
            P("dp", None, "tp"),
            P("dp", None, "tp"),
            P("dp", "seq", "tp"),
            P("dp", None, "seq"),
            P("dp", None),
            P("seq"),
            P("seq", "tp"),
            P("seq", "tp"),
            P("seq", None),
            P(None, "tp"),
            P("seq", None),
            P(None, "tp"),
            P("tp", "seq"),
        ),
        out_specs=(
            P("dp", "seq", "tp"),
            P("dp", None, "seq"),
            P("dp", "seq", "tp"),
            P("seq", None),
            P(None, "tp"),
            P("seq", None),
            P(None, "tp"),
        ),
        check_vma=False,
    )
```

profile of v0, /device:TPU:0, one launch (start us, length us, event | category | flops | bytes accessed | tf_op | source)
XLA Modules:
  0.0 260.0 jit_solution(13996645604711134509)
XLA Ops:
  0.6 1.5 copy.21.scale
  2.2 0.0 copy-start.2
  2.2 0.9 copy-done.2
  3.1 0.0 copy-start.3
  3.1 0.9 copy-done.3
  4.0 134.8 %attention.1 = (bf16[512,2560]{1,0:T(8,128)(2,1)S(1)}, bf16[512,2560]{1,0:T(8,128)(2,1)}, bf16[512,2560]{1,0:T(8,128)(2,1)}, bf16[512,1024]{1,0:T(8,128)(2,1)S(1)}, bf16[512,64]{1,0:T(8,128)(2,1)S(1)}) custom-call(bf16[512,2560]{1,0:T(8,128)(2,1)} %bitcast.24, bf16[512,2560]{1,0:T(8,128)(2,1)} %bitcast.25, bf16[512,2560]{1,0:T(8,128)(2,1)} %bitcast.26, ...), custom_call_target="tpu_custom_call" | custom-call | flops 9395240960 | bytes 15728640 | tf_op jit(solution)/shard_map/attention/pallas_call | solution.py:212
  138.8 0.0 copy-start
  138.8 1.0 copy-done
  139.8 0.0 copy-start.1
  139.8 0.7 copy-done.1
  140.4 112.9 %tail.1 = (bf16[512,1024]{1,0:T(8,128)(2,1)}, bf16[128,5120]{1,0:T(8,128)(2,1)}, f32[32,1024]{1,0:T(8,128)}, f32[32,1024]{1,0:T(8,128)}, f32[32,2560]{1,0:T(8,128)}, /*index=5*/f32[32,2560]{1,0:T(8,128)}) custom-call(bf16[512,1024]{1,0:T(8,128)(2,1)} %copy-done, bf16[512,64]{1,0:T(8,128)(2,1)} %copy-done.1, bf16[512,1024]{1,0:T(8,128)(2,1)} %bitcast.16, ...), custom_call_target="tpu_custom_call" | custom-call | tf_op jit(solution)/shard_map/tail/pallas_call | solution.py:630
  253.3 0.0 copy-start.5
  253.3 0.0 copy-start.4
  253.3 1.5 copy.29
  254.8 0.4 copy-done.5
  255.2 0.0 copy-start.9
  255.2 0.0 copy-start.7
  255.2 0.0 copy-start.8
  255.2 0.0 copy-start.6
  255.2 1.0 copy.30
  256.2 0.0 copy-done.4
  256.2 1.1 copy.31
  257.3 0.0 copy-done.9
  257.3 0.7 copy.32
  257.9 0.0 copy-done.7
  257.9 0.7 copy.33
  258.6 0.0 copy-done.8
  258.6 0.7 copy.34
  259.3 0.0 copy-done.6
  259.3 0.7 copy.35
Async XLA Ops:
  2.2 0.9 copy-start.2
  3.1 0.9 copy-start.3
  138.8 1.0 copy-start
  139.8 0.7 copy-start.1
  253.3 1.9 copy-start.5
  253.3 2.9 %copy-start.4 = (bf16[128,5120]{1,0:T(8,128)(2,1)S(1)}, bf16[128,5120]{1,0:T(8,128)(2,1)}, u32[]{:S(2)}) copy-start(bf16[128,5120]{1,0:T(8,128)(2,1)} %get-tuple-element.24) | copy-start | bytes 3932164
  255.2 2.0 copy-start.9
  255.2 2.7 %copy-start.7 = (f32[32,2560]{1,0:T(8,128)S(1)}, f32[32,2560]{1,0:T(8,128)}, u32[]{:S(2)}) copy-start(f32[32,2560]{1,0:T(8,128)} %get-tuple-element.40) | copy-start | bytes 983044
  255.2 3.4 %copy-start.8 = (f32[32,1024]{1,0:T(8,128)S(1)}, f32[32,1024]{1,0:T(8,128)}, u32[]{:S(2)}) copy-start(f32[32,1024]{1,0:T(8,128)} %get-tuple-element.27) | copy-start | bytes 393220
  255.2 4.1 %copy-start.6 = (f32[32,2560]{1,0:T(8,128)S(1)}, f32[32,2560]{1,0:T(8,128)}, u32[]{:S(2)}) copy-start(f32[32,2560]{1,0:T(8,128)} %get-tuple-element.42) | copy-start | bytes 983044
where the time goes:
time: 260 us
  Pallas kernels  248 us (95%)
  local copies, waits for them, and re-layouts  11.7 us (4%)
    pallas_call x1, Pallas kernels, attention_grads(): pl.pallas_call(functools.partial(attention_kernel, n, heads, lag), grid=(...  135 us
    pallas_call x1, Pallas kernels, tail(): pl.pallas_call(functools.partial(tail_kernel, n, splits, prompts, slices,...  113 us
    unnamed x27, local copies, waits for them, and re-layouts  10.2 us

commit v1 on v0

v1 whole, which is shorter than its diff:
```python
import functools

import jax
import jax.numpy as jnp
from jax import lax
from jax.experimental import pallas as pl
from jax.experimental.pallas import tpu as pltpu
from jax.sharding import PartitionSpec as P

HD = 128
MESH = pl.DeviceIdType.MESH
LOW = jnp.bfloat16


def dot(left_side, right_side, left_dim, right_dim):
    return lax.dot_general(
        left_side,
        right_side,
        (((left_dim,), (right_dim,)), ((), ())),
        preferred_element_type=jnp.float32,
    )


def exchange(axis, size, landing, send, recv):
    me = lax.axis_index(axis)

    def copy(slot, offset):
        return pltpu.make_async_remote_copy(
            src_ref=landing.at[slot],
            dst_ref=landing.at[slot],
            send_sem=send.at[offset],
            recv_sem=recv.at[slot],
            device_id={axis: lax.rem(me + offset, size)},
            device_id_type=MESH,
        )

    def start():
        for offset in range(1, size):
            copy(me, offset).start()

    def finish():
        for offset in range(1, size):
            copy(lax.rem(me + offset, size), offset).wait_recv()
        for offset in range(1, size):
            copy(me, offset).wait_send()

    return start, finish


def low_sum(ref, size):
    value = ref[0].astype(jnp.float32)
    for index in range(1, size):
        value = value + ref[index].astype(jnp.float32)
    return value


def kernel(
    plan,
    queries,
    keys,
    values,
    grads,
    key_weight,
    value_weight,
    key_up,
    value_up,
    out_weight,
    normed,
    scale,
    gain,
    key_down,
    value_down,
    grad_query,
    grad_hidden,
    grad_text,
    key_down_grad,
    value_down_grad,
    key_up_grad,
    value_up_grad,
    part,
    up_in,
    up_out,
    down_in,
    down_out,
    total,
    project,
    context_all,
    project_all,
    text,
    sum_all,
    latent_own,
    latent_all,
    latent,
    up_sum,
    up_all,
    rows_all,
    down_sum,
    down_all,
    up_send,
    up_recv,
    down_send,
    down_recv,
    high_send,
    high_recv,
    low_send,
    low_recv,
    context_send,
    context_recv,
    project_send,
    project_recv,
    sum_send,
    sum_recv,
    latent_send,
    latent_recv,
    up_dp_send,
    up_dp_recv,
    down_dp_send,
    down_dp_recv,
    rows_send,
    rows_recv,
    text_sem,
):
    n, splits, prompts = plan["n"], plan["splits"], plan["prompts"]
    heads, slices, lag = plan["heads"], plan["slices"], plan["lag"]
    first, second, steps = plan["first"], plan["second"], plan["steps"]
    length, features = normed.shape
    block = length // n
    sub = block // 2
    half_length = length // 2
    rank = key_down.shape[0]
    step = pl.program_id(0)
    me = lax.axis_index("seq")
    split = lax.axis_index("tp")
    prompt = lax.axis_index("dp")
    factor = HD ** (-0.5)
    above = lax.rem(me + 1, n)
    below = lax.rem(me + n - 1, n)
    has_low = me > 0
    has_high = me < n - 1

    def rows_of(value, half):
        return jnp.concatenate(
            [
                value[owner * block + half * sub : owner * block + half * sub + sub]
                for owner in range(n)
            ],
            axis=0,
        )

    def context_of(half):
        return (rows_of(normed, half).astype(jnp.float32) * gain[...]).astype(LOW)

    def column(row, size):
        return jnp.transpose(jnp.broadcast_to(row, (128, size)))[:, :1]

    def up_copy(half, index, source):
        return pltpu.make_async_remote_copy(
            src_ref=source.at[half, index],
            dst_ref=up_in.at[half, index],
            send_sem=up_send.at[half, index],
            recv_sem=up_recv.at[half, index],
            device_id={"seq": above},
            device_id_type=MESH,
        )

    def down_copy(half, index, source):
        return pltpu.make_async_remote_copy(
            src_ref=source.at[half, index],
            dst_ref=down_in.at[half, index],
            send_sem=down_send.at[half, index],
            recv_sem=down_recv.at[half, index],
            device_id={"seq": below},
            device_id_type=MESH,
        )

    def high_copy(half, index, source, owner):
        rows = pl.ds(owner * sub, (n - owner) * sub)
        return pltpu.make_async_remote_copy(
            src_ref=source.at[half, index, :, rows],
            dst_ref=up_in.at[half, index, :, rows],
            send_sem=high_send.at[half, index],
            recv_sem=high_recv.at[half, index],
            device_id={"seq": above},
            device_id_type=MESH,
        )

    def low_copy(half, index, source, owner):
        rows = pl.ds(0, (owner + 1) * sub)
        return pltpu.make_async_remote_copy(
            src_ref=source.at[half, index, :, rows],
            dst_ref=down_in.at[half, index, :, rows],
            send_sem=low_send.at[half, index],
            recv_sem=low_recv.at[half, index],
            device_id={"seq": below},
            device_id_type=MESH,
        )

    def attend(position):
        live = jnp.logical_and(position >= 0, position < 2 * heads)
        half = (position >= heads).astype(jnp.int32)
        return live, half, position - half * heads

    def hide(position):
        live = jnp.logical_or(
            jnp.logical_and(position >= first, position < first + slices),
            jnp.logical_and(position >= second, position < second + slices),
        )
        half = (position >= second).astype(jnp.int32)
        return live, half, position - first - half * (second - first)

    @pl.when(step == 0)
    def _():
        barrier = pltpu.get_barrier_semaphore()
        for axis, size in (("tp", splits), ("seq", n), ("dp", prompts)):
            for offset in range(1, size):
                pl.semaphore_signal(
                    barrier,
                    inc=1,
                    device_id={axis: lax.rem(lax.axis_index(axis) + offset, size)},
                    device_id_type=MESH,
                )
        pl.semaphore_wait(barrier, splits + n + prompts - 3)

    @pl.when(step < heads)
    def _():
        query, key, value, grad = queries[...], keys[...], values[...], grads[...]
        scores = dot(key, query, 1, 1) * factor
        weights = jnp.exp(scores - jnp.max(scores, axis=0, keepdims=True))
        probability = weights * (1.0 / jnp.sum(weights, axis=0, keepdims=True))
        value_part = dot(probability.astype(LOW), grad, 1, 0).astype(LOW)
        grad_probs = dot(value, grad, 1, 1)
        grad_scores = probability * (
            grad_probs - jnp.sum(probability * grad_probs, axis=0, keepdims=True)
        )
        grad_low = grad_scores.astype(LOW)
        key_part = (dot(grad_low, query, 1, 0) * factor).astype(LOW)
        for kind, side in ((0, key_part), (1, value_part)):
            for half in range(2):
                part[half, step, kind] = rows_of(side, half)
        grad_query[...] = (dot(grad_low, key, 0, 0) * factor).astype(LOW)

    live, half, index = hide(step)

    @pl.when(live)
    def _():
        product = dot(text[half].reshape(half_length, features), out_weight[...], 1, 1)
        product = product.astype(LOW)
        part[half, index, 0] = product[:, :HD]
        part[half, index, 1] = product[:, HD:]

    up_at = step - 2 * me
    down_at = step - 2 * (n - 1 - me)

    live, half, index = attend(up_at)

    @pl.when(jnp.logical_and(live, me == 0))
    def _():
        up_copy(half, index, part).start()
        up_in[half, index] = jnp.zeros(up_in.shape[2:], LOW)

    @pl.when(jnp.logical_and(live, has_low))
    def _():
        up_copy(half, index, up_out).wait_recv()

        @pl.when(has_high)
        def _():
            up_out[half, index] = up_in[half, index] + part[half, index]
            up_copy(half, index, up_out).start()

    live, half, index = attend(down_at)

    @pl.when(jnp.logical_and(live, me == n - 1))
    def _():
        down_copy(half, index, part).start()
        down_in[half, index] = jnp.zeros(down_in.shape[2:], LOW)

    @pl.when(jnp.logical_and(live, has_high))
    def _():
        down_copy(half, index, down_out).wait_recv()

        @pl.when(has_low)
        def _():
            down_out[half, index] = down_in[half, index] + part[half, index]
            down_copy(half, index, down_out).start()

    live, half, index = hide(up_at)
    for place in range(n):

        @pl.when(jnp.logical_and(live, me == place))
        def _():
            if place > 0:
                high_copy(half, index, up_out, place).wait_recv()
            else:
                up_in[half, index, :, :sub] = jnp.zeros((2, sub, HD), LOW)
            if place < n - 1:
                rest = (place + 1) * sub
                if place > 0:
                    up_out[half, index, :, rest:] = (
                        up_in[half, index, :, rest:] + part[half, index, :, rest:]
                    )
                high_copy(half, index, up_out if place > 0 else part, place + 1).start()

    live, half, index = hide(down_at)
    for place in range(n):

        @pl.when(jnp.logical_and(live, me == place))
        def _():
            if place < n - 1:
                low_copy(half, index, down_out, place).wait_recv()
            else:
                down_in[half, index, :, place * sub :] = jnp.zeros((2, sub, HD), LOW)
            if place > 0:
                rest = place * sub
                if place < n - 1:
                    down_out[half, index, :, :rest] = (
                        down_in[half, index, :, :rest] + part[half, index, :, :rest]
                    )
                low_copy(half, index, down_out if place < n - 1 else part, place - 1).start()

    @pl.when(step == 0)
    def _():
        total[...] = jnp.zeros_like(total)
        project[...] = jnp.zeros_like(project)
        up_sum[...] = jnp.zeros_like(up_sum)

    def latent_copy(slot, owner, offset):
        return pltpu.make_async_remote_copy(
            src_ref=latent_own.at[owner],
            dst_ref=latent_all.at[slot],
            send_sem=latent_send.at[offset],
            recv_sem=latent_recv.at[slot],
            device_id={"seq": lax.rem(me + offset, n)},
            device_id_type=MESH,
        )

    @pl.when(step == 1)
    def _():
        down = jnp.concatenate([key_down[...], value_down[...]], axis=0)
        sides = [dot(down, context_of(side), 1, 1) for side in range(2)]
        latent_own[...] = (
            jnp.concatenate(sides, axis=1).reshape(latent_own.shape).astype(LOW)
        )
        for offset in range(1, n):
            latent_copy(me, lax.rem(me + offset, n), offset).start()
        latent_all[me] = latent_own[me]

    @pl.when(step == lag - 1)
    def _():
        for offset in range(1, n):
            latent_copy(lax.rem(me + offset, n), me, offset).wait_recv()
        for offset in range(1, n):
            latent_copy(me, lax.rem(me + offset, n), offset).wait_send()
        both = low_sum(latent_all, n).astype(LOW)
        for side in range(2):
            latent[side] = both[:, side * half_length : (side + 1) * half_length]

    live, half, index = attend(step - lag)

    @pl.when(live)
    def _():
        @pl.when(has_high)
        def _():
            up_copy(half, index, up_out).wait_send()

        @pl.when(has_low)
        def _():
            down_copy(half, index, down_out).wait_send()

        both = (
            up_in[half, index].astype(jnp.float32)
            + part[half, index].astype(jnp.float32)
            + down_in[half, index].astype(jnp.float32)
        ).astype(LOW)
        pair = jnp.concatenate([both[0], both[1]], axis=1)
        slab = jnp.concatenate([key_weight[...], value_weight[...]], axis=1)
        total[half] += dot(pair, slab, 1, 1)
        blank = jnp.zeros((rank, HD), LOW)
        rises = jnp.concatenate(
            [
                jnp.concatenate([key_up[...], blank], axis=1),
                jnp.concatenate([blank, value_up[...]], axis=1),
            ],
            axis=0,
        )
        project[half] += dot(pair, rises, 1, 1)
        own = jnp.where(me < n // 2, both[0], both[1])
        up_sum[index] += dot(latent[half], own, 1, 0)

    for side in range(2):
        end = heads * (side + 1) + lag - 1
        project_start, project_finish = exchange(
            "tp", splits, project_all.at[side], project_send.at[side], project_recv.at[side]
        )
        context_start, context_finish = exchange(
            "tp", splits, context_all.at[side], context_send.at[side], context_recv.at[side]
        )
        sum_start, sum_finish = exchange(
            "seq", n, sum_all.at[side], sum_send.at[side], sum_recv.at[side]
        )

        @pl.when(step == end)
        def _():
            project_all[side, split] = project[side].astype(LOW)
            context_all[side, split] = total[side].astype(LOW)
            project_start()
            context_start()

        @pl.when(step == end + 2)
        def _():
            project_finish()
            context_finish()
            back = low_sum(project_all.at[side], splits).astype(LOW)
            low_rank = dot(back[:, :rank], key_down[...], 1, 0) + dot(
                back[:, rank:], value_down[...], 1, 0
            )
            scaled = gain[...] * (low_sum(context_all.at[side], splits) + low_rank)
            total[side] = scaled
            local_sum = jnp.sum(
                rows_of(normed, side).astype(jnp.float32) * scaled, axis=1, keepdims=True
            )
            sum_all[side, me] = jnp.transpose(jnp.broadcast_to(local_sum, (half_length, 128)))[
                :8, :
            ]
            sum_start()
            down = dot(back, context_of(side), 0, 0)
            if side == 0:
                down_sum[...] = down
            else:
                down_sum[...] += down

        @pl.when(step == end + 6)
        def _():
            sum_finish()
            token_sum = sum_all[side, 0]
            for other in range(1, n):
                token_sum = token_sum + sum_all[side, other]
            token_column = column(token_sum[:1, :], half_length)
            result = rows_of(column(scale[...], length), side) * (
                total[side]
                - rows_of(normed, side).astype(jnp.float32)
                * (token_column / plan["features_whole"])
            )
            text[side] = result.astype(LOW).reshape(n, sub, features)
            for owner in range(n):
                pltpu.make_async_copy(
                    text.at[side, owner],
                    grad_text.at[pl.ds(owner * block + side * sub, sub)],
                    text_sem.at[side, owner],
                ).start()

    end = 2 * heads + lag - 1
    up_start, up_finish = exchange("dp", prompts, up_all, up_dp_send, up_dp_recv)
    down_start, down_finish = exchange("dp", prompts, down_all, down_dp_send, down_dp_recv)
    rows_start, rows_finish = exchange("seq", n, rows_all, rows_send, rows_recv)

    @pl.when(step == end + 1)
    def _():
        up_all[prompt] = jnp.concatenate(
            [up_sum[index] for index in range(heads)], axis=1
        ).astype(LOW)
        up_start()

    @pl.when(step == end + 3)
    def _():
        down_all[prompt] = down_sum[...].astype(LOW)
        down_start()

    @pl.when(step == end + 7)
    def _():
        up_finish()
        rows_all[me] = (low_sum(up_all, prompts) / prompts).astype(LOW)
        rows_start()

    @pl.when(step == end + 9)
    def _():
        down_finish()
        down = low_sum(down_all, prompts)
        key_down_grad[...] = down[:rank] / prompts
        value_down_grad[...] = down[rank:] / prompts

    @pl.when(step == end + 14)
    def _():
        rows_finish()
        key_up_grad[...] = rows_all[: n // 2].astype(jnp.float32).reshape(key_up_grad.shape)
        value_up_grad[...] = rows_all[n // 2 :].astype(jnp.float32).reshape(value_up_grad.shape)

    live, half, index = hide(step - lag)
    for place in range(n):

        @pl.when(jnp.logical_and(live, me == place))
        def _():
            if place < n - 1:
                high_copy(half, index, up_out, place + 1).wait_send()
            if place > 0:
                low_copy(half, index, down_out, place - 1).wait_send()
            own = slice(place * sub, (place + 1) * sub)
            both = (
                up_in[half, index, :, own].astype(jnp.float32)
                + part[half, index, :, own].astype(jnp.float32)
                + down_in[half, index, :, own].astype(jnp.float32)
            ).astype(LOW)
            grad_hidden[...] = jnp.concatenate([both[0], both[1]], axis=1)

    @pl.when(step == steps - 1)
    def _():
        for side in range(2):
            for owner in range(n):
                pltpu.make_async_copy(
                    text.at[side, owner],
                    grad_text.at[pl.ds(owner * block + side * sub, sub)],
                    text_sem.at[side, owner],
                ).wait()


def shards(
    queries,
    keys,
    values,
    grad_attention,
    normed,
    norm_scale,
    norm_gain,
    key_weight,
    value_weight,
    key_down,
    key_up,
    value_down,
    value_up,
    out_weight,
):
    rows, columns = queries.shape[1:]
    length, features = normed.shape[1:]
    rank = key_up.shape[0]
    hidden = out_weight.shape[0]
    n, splits, prompts = lax.axis_size("seq"), lax.axis_size("tp"), lax.axis_size("dp")
    heads = columns // HD
    width = 2 * HD
    slices = hidden // width
    lag = 2 * (n - 1)
    first = max(2 * heads, heads + lag + 6)
    second = max(first + slices, 2 * heads + lag + 6)
    steps = max(second + slices + lag, 2 * heads + lag + 14)
    block = length // n
    sub = block // 2
    half_length = length // 2
    share = 2 * rank // n
    plan = dict(
        n=n,
        splits=splits,
        prompts=prompts,
        heads=heads,
        slices=slices,
        lag=lag,
        first=first,
        second=second,
        steps=steps,
        features_whole=features * n,
    )

    def early(height):
        return pl.BlockSpec((height, HD), lambda step: (0, jnp.minimum(step, heads - 1)))

    def late(height):
        def place(step):
            at = jnp.clip(step - lag, 0, 2 * heads - 1)
            return 0, at - jnp.where(at >= heads, heads, 0)

        return pl.BlockSpec((height, HD), place)

    def fixed(height, size):
        return pl.BlockSpec((height, size), lambda step: (0, 0))

    def slice_of(step):
        after = step >= second
        return after.astype(jnp.int32), jnp.clip(
            step - jnp.where(after, second, first), 0, slices - 1
        )

    buffer = pltpu.VMEM((2, max(heads, slices), 2, half_length, HD), LOW)
    dma = pltpu.SemaphoreType.DMA
    grad_query, grad_hidden, grad_text, down_key, down_value, up_key, up_value = pl.pallas_call(
        functools.partial(kernel, plan),
        grid=(steps,),
        out_shape=(
            jax.ShapeDtypeStruct((rows, columns), LOW),
            jax.ShapeDtypeStruct((block, hidden), LOW),
            jax.ShapeDtypeStruct((length, features), LOW),
            jax.ShapeDtypeStruct((rank, features), jnp.float32),
            jax.ShapeDtypeStruct((rank, features), jnp.float32),
            jax.ShapeDtypeStruct((rank, columns), jnp.float32),
            jax.ShapeDtypeStruct((rank, columns), jnp.float32),
        ),
        in_specs=[
            early(rows),
            early(length),
            early(length),
            early(rows),
            late(features),
            late(features),
            late(rank),
            late(rank),
            pl.BlockSpec((width, features), lambda step: (slice_of(step)[1], 0)),
            fixed(length, features),
            fixed(1, length),
            fixed(1, features),
            fixed(rank, features),
            fixed(rank, features),
        ],
        out_specs=(
            early(rows),
            pl.BlockSpec((sub, width), lambda step: slice_of(step - lag)),
            pl.BlockSpec(memory_space=pl.ANY),
            fixed(rank, features),
            fixed(rank, features),
            fixed(rank, columns),
            fixed(rank, columns),
        ),
        scratch_shapes=[buffer] * 5
        + [
            pltpu.VMEM((2, half_length, features), jnp.float32),
            pltpu.VMEM((2, half_length, 2 * rank), jnp.float32),
            pltpu.VMEM((2, splits, half_length, features), LOW),
            pltpu.VMEM((2, splits, half_length, 2 * rank), LOW),
            pltpu.VMEM((2, n, sub, features), LOW),
            pltpu.VMEM((2, n, 8, half_length), jnp.float32),
            pltpu.VMEM((n, share, length), LOW),
            pltpu.VMEM((n, share, length), LOW),
            pltpu.VMEM((2, share, half_length), LOW),
            pltpu.VMEM((heads, share, HD), jnp.float32),
            pltpu.VMEM((prompts, share, columns), LOW),
            pltpu.VMEM((n, share, columns), LOW),
            pltpu.VMEM((2 * rank, features), jnp.float32),
            pltpu.VMEM((prompts, 2 * rank, features), LOW),
        ]
        + [dma((2, heads))] * 4
        + [dma((2, slices))] * 4
        + [dma((2, splits))] * 4
        + [dma((2, n))] * 2
        + [dma((n,))] * 2
        + [dma((prompts,))] * 4
        + [dma((n,))] * 2
        + [dma((2, n))],
        compiler_params=pltpu.CompilerParams(
            collective_id=0, has_side_effects=True, vmem_limit_bytes=62 * 1024 * 1024
        ),
        name="fused",
    )(
        queries[0],
        keys[0],
        values[0],
        grad_attention[0],
        key_weight,
        value_weight,
        key_up,
        value_up,
        out_weight,
        normed[0],
        norm_scale,
        norm_gain[None, :],
        key_down.T,
        value_down.T,
    )
    return (
        grad_query[None],
        grad_text[None],
        grad_hidden[None],
        down_key.T,
        up_key,
        down_value.T,
        up_value,
    )


def solution(mesh):
    return jax.shard_map(
        shards,
        mesh=mesh,
        in_specs=(
            P("dp", "seq", "tp"),
            P("dp", None, "tp"),
            P("dp", None, "tp"),
            P("dp", "seq", "tp"),
            P("dp", None, "seq"),
            P("dp", None),
            P("seq"),
            P("seq", "tp"),
            P("seq", "tp"),
            P("seq", None),
            P(None, "tp"),
            P("seq", None),
            P(None, "tp"),
            P("tp", "seq"),
        ),
        out_specs=(
            P("dp", "seq", "tp"),
            P("dp", None, "seq"),
            P("dp", "seq", "tp"),
            P("seq", None),
            P(None, "tp"),
            P("seq", None),
            P(None, "tp"),
        ),
        check_vma=False,
    )
```

time: 260 us -> 237 us (0.912)
  Pallas kernels: 248 us -> 228 us
  local copies, waits for them, and re-layouts: 11.7 us -> 8.36 us
    pallas_call x2 -> x1, Pallas kernels: 248 us -> 228 us  [shards(): pl.pallas_call(functools.partial(kernel, plan), grid=(steps,), out_shape=...]
    unnamed x27 -> x19, local copies, waits for them, and re-layouts: 10.2 us -> 8.36 us
where the time goes in v1:
time: 237 us
  Pallas kernels  228 us (96%)
  local copies, waits for them, and re-layouts  8.36 us (4%)
    pallas_call x1, Pallas kernels, shards(): pl.pallas_call(functools.partial(kernel, plan), grid=(steps,), out_shape=...  228 us
    unnamed x19, local copies, waits for them, and re-layouts  8.36 us

profile of v1, /device:TPU:0, one launch (start us, length us, event | category | flops | bytes accessed | tf_op | source)
XLA Modules:
  0.0 236.6 jit_solution(10518428525143166699)
XLA Ops:
  0.6 227.6 %fused.1 = (bf16[512,2560]{1,0:T(8,128)(2,1)}, bf16[128,5120]{1,0:T(8,128)(2,1)}, bf16[512,1024]{1,0:T(8,128)(2,1)}, f32[32,1024]{1,0:T(8,128)}, f32[32,1024]{1,...) custom-call(bf16[512,2560]{1,0:T(8,128)(2,1)} %bitcast.13, bf16[512,2560]{1,0:T(8,128)(2,1)} %bitcast.14, ...), custom_call_target="tpu_custom_call" | custom-call | tf_op jit(solution)/shard_map/fused/pallas_call | solution.py:581
  228.2 0.0 copy-start.1
  228.2 0.0 copy-start
  228.2 3.6 %copy.28 = bf16[1,512,2560]{2,1,0:T(8,128)(2,1)} copy(bf16[1,512,2560]{2,1,0:T(8,128)(2,1)} %bitcast.17) | data formatting | bytes 5242880
  231.8 0.0 copy-done.1
  231.8 0.0 copy-start.5
  231.8 0.0 copy-start.3
  231.8 0.0 copy-start.4
  231.8 0.0 copy-start.2
  231.8 1.0 copy.29
  232.8 0.0 copy-done
  232.8 1.1 copy.30
  233.8 0.0 copy-done.5
  233.8 0.7 copy.31
  234.5 0.0 copy-done.3
  234.5 0.7 copy.32
  235.2 0.0 copy-done.4
  235.2 0.7 copy.33
  235.9 0.0 copy-done.2
  235.9 0.7 copy.34
Async XLA Ops:
  228.2 3.6 %copy-start.1 = (bf16[512,1024]{1,0:T(8,128)(2,1)S(1)}, bf16[512,1024]{1,0:T(8,128)(2,1)}, u32[]{:S(2)}) copy-start(bf16[512,1024]{1,0:T(8,128)(2,1)} %get-tuple-element.15) | copy-start | bytes 3145732
  228.2 4.6 %copy-start = (bf16[128,5120]{1,0:T(8,128)(2,1)S(1)}, bf16[128,5120]{1,0:T(8,128)(2,1)}, u32[]{:S(2)}) copy-start(bf16[128,5120]{1,0:T(8,128)(2,1)} %get-tuple-element.16) | copy-start | bytes 3932164
  231.8 2.1 copy-start.5
  231.8 2.7 %copy-start.3 = (f32[32,2560]{1,0:T(8,128)S(1)}, f32[32,2560]{1,0:T(8,128)}, u32[]{:S(2)}) copy-start(f32[32,2560]{1,0:T(8,128)} %get-tuple-element.32) | copy-start | bytes 983044
  231.8 3.4 %copy-start.4 = (f32[32,1024]{1,0:T(8,128)S(1)}, f32[32,1024]{1,0:T(8,128)}, u32[]{:S(2)}) copy-start(f32[32,1024]{1,0:T(8,128)} %get-tuple-element.19) | copy-start | bytes 393220
  231.8 4.1 %copy-start.2 = (f32[32,2560]{1,0:T(8,128)S(1)}, f32[32,2560]{1,0:T(8,128)}, u32[]{:S(2)}) copy-start(f32[32,2560]{1,0:T(8,128)} %get-tuple-element.34) | copy-start | bytes 983044

commit v2 on v1

--- a/solution.py
+++ b/solution.py
@@ -92,8 +92,10 @@
     latent_all,
     latent,
     up_sum,
+    up_own,
     up_all,
     rows_all,
+    up_whole,
     down_sum,
     down_all,
     up_send,
@@ -118,6 +120,12 @@
     down_dp_recv,
     rows_send,
     rows_recv,
+    whole_send,
+    whole_recv,
+    near_up_send,
+    near_up_recv,
+    near_down_send,
+    near_down_recv,
     text_sem,
 ):
     n, splits, prompts = plan["n"], plan["splits"], plan["prompts"]
@@ -195,6 +203,28 @@
             device_id_type=MESH,
         )
 
+    def near_up_copy(half, index):
+        rows = pl.ds(sub, sub)
+        return pltpu.make_async_remote_copy(
+            src_ref=part.at[half, index, :, rows],
+            dst_ref=up_in.at[half, index, :, rows],
+            send_sem=near_up_send.at[half, index],
+            recv_sem=near_up_recv.at[half, index],
+            device_id={"seq": above},
+            device_id_type=MESH,
+        )
+
+    def near_down_copy(half, index):
+        rows = pl.ds((n - 2) * sub, sub)
+        return pltpu.make_async_remote_copy(
+            src_ref=part.at[half, index, :, rows],
+            dst_ref=down_in.at[half, index, :, rows],
+            send_sem=near_down_send.at[half, index],
+            recv_sem=near_down_recv.at[half, index],
+            device_id={"seq": below},
+            device_id_type=MESH,
+        )
+
     def attend(position):
         live = jnp.logical_and(position >= 0, position < 2 * heads)
         half = (position >= heads).astype(jnp.int32)
@@ -219,7 +249,6 @@
                     device_id={axis: lax.rem(lax.axis_index(axis) + offset, size)},
                     device_id_type=MESH,
                 )
-        pl.semaphore_wait(barrier, splits + n + prompts - 3)
 
     @pl.when(step < heads)
     def _():
@@ -239,6 +268,10 @@
                 part[half, step, kind] = rows_of(side, half)
         grad_query[...] = (dot(grad_low, key, 0, 0) * factor).astype(LOW)
 
+    @pl.when(step == 0)
+    def _():
+        pl.semaphore_wait(pltpu.get_barrier_semaphore(), splits + n + prompts - 3)
+
     live, half, index = hide(step)
 
     @pl.when(live)
@@ -288,34 +321,52 @@
 
         @pl.when(jnp.logical_and(live, me == place))
         def _():
-            if place > 0:
+            if place == 0:
+                up_in[half, index, :, :sub] = jnp.zeros((2, sub, HD), LOW)
+                if n > 2:
+                    high_copy(half, index, part, 2).start()
+            elif place == 1:
+                if n > 2:
+                    high_copy(half, index, up_out, 2).wait_recv()
+            else:
                 high_copy(half, index, up_out, place).wait_recv()
-            else:
-                up_in[half, index, :, :sub] = jnp.zeros((2, sub, HD), LOW)
-            if place < n - 1:
+            if 0 < place < n - 1:
                 rest = (place + 1) * sub
-                if place > 0:
-                    up_out[half, index, :, rest:] = (
-                        up_in[half, index, :, rest:] + part[half, index, :, rest:]
-                    )
-                high_copy(half, index, up_out if place > 0 else part, place + 1).start()
+                up_out[half, index, :, rest:] = (
+                    up_in[half, index, :, rest:] + part[half, index, :, rest:]
+                )
+                high_copy(half, index, up_out, place + 1).start()
 
     live, half, index = hide(down_at)
     for place in range(n):
 
         @pl.when(jnp.logical_and(live, me == place))
         def _():
-            if place < n - 1:
+            if place == n - 1:
+                down_in[half, index, :, place * sub :] = jnp.zeros((2, sub, HD), LOW)
+                if n > 2:
+                    low_copy(half, index, part, n - 3).start()
+            elif place == n - 2:
+                if n > 2:
+                    low_copy(half, index, down_out, n - 3).wait_recv()
+            else:
                 low_copy(half, index, down_out, place).wait_recv()
-            else:
-                down_in[half, index, :, place * sub :] = jnp.zeros((2, sub, HD), LOW)
-            if place > 0:
+            if 0 < place < n - 1:
                 rest = place * sub
-                if place < n - 1:
-                    down_out[half, index, :, :rest] = (
-                        down_in[half, index, :, :rest] + part[half, index, :, :rest]
-                    )
-                low_copy(half, index, down_out if place < n - 1 else part, place - 1).start()
+                down_out[half, index, :, :rest] = (
+                    down_in[half, index, :, :rest] + part[half, index, :, :rest]
+                )
+                low_copy(half, index, down_out, place - 1).start()
+
+    live, half, index = hide(step - plan["delay"])
+
+    @pl.when(jnp.logical_and(live, me == 0))
+    def _():
+        near_up_copy(half, index).start()
+
+    @pl.when(jnp.logical_and(live, me == n - 1))
+    def _():
+        near_down_copy(half, index).start()
 
     @pl.when(step == 0)
     def _():
@@ -418,9 +469,10 @@
             local_sum = jnp.sum(
                 rows_of(normed, side).astype(jnp.float32) * scaled, axis=1, keepdims=True
             )
-            sum_all[side, me] = jnp.transpose(jnp.broadcast_to(local_sum, (half_length, 128)))[
-                :8, :
-            ]
+            line = jnp.transpose(jnp.broadcast_to(local_sum, (half_length, 128)))[:1, :]
+            sum_all[side, me] = jnp.concatenate(
+                [line[:, at : at + 128] for at in range(0, half_length, 128)], axis=0
+            )
             sum_start()
             down = dot(back, context_of(side), 0, 0)
             if side == 0:
@@ -434,7 +486,10 @@
             token_sum = sum_all[side, 0]
             for other in range(1, n):
                 token_sum = token_sum + sum_all[side, other]
-            token_column = column(token_sum[:1, :], half_length)
+            line = jnp.concatenate(
+                [token_sum[at : at + 1] for at in range(half_length // 128)], axis=1
+            )
+            token_column = column(line, half_length)
             result = rows_of(column(scale[...], length), side) * (
                 total[side]
                 - rows_of(normed, side).astype(jnp.float32)
@@ -449,25 +504,42 @@
                 ).start()
 
     end = 2 * heads + lag - 1
-    up_start, up_finish = exchange("dp", prompts, up_all, up_dp_send, up_dp_recv)
+    portion = up_own.shape[2]
+
+    def up_piece(slot, owner, offset):
+        return pltpu.make_async_remote_copy(
+            src_ref=up_own.at[owner],
+            dst_ref=up_all.at[slot],
+            send_sem=up_dp_send.at[offset],
+            recv_sem=up_dp_recv.at[slot],
+            device_id={"dp": lax.rem(prompt + offset, prompts)},
+            device_id_type=MESH,
+        )
+
+    whole_start, whole_finish = exchange("dp", prompts, up_whole, whole_send, whole_recv)
     down_start, down_finish = exchange("dp", prompts, down_all, down_dp_send, down_dp_recv)
     rows_start, rows_finish = exchange("seq", n, rows_all, rows_send, rows_recv)
 
     @pl.when(step == end + 1)
     def _():
-        up_all[prompt] = jnp.concatenate(
-            [up_sum[index] for index in range(heads)], axis=1
-        ).astype(LOW)
-        up_start()
+        rows = jnp.concatenate([up_sum[index] for index in range(heads)], axis=1).astype(LOW)
+        for owner in range(prompts):
+            up_own[owner] = rows[:, owner * portion : (owner + 1) * portion]
+        for offset in range(1, prompts):
+            up_piece(prompt, lax.rem(prompt + offset, prompts), offset).start()
+        up_all[prompt] = up_own[prompt]
 
     @pl.when(step == end + 3)
     def _():
         down_all[prompt] = down_sum[...].astype(LOW)
         down_start()
 
-    @pl.when(step == end + 7)
-    def _():
-        up_finish()
+    @pl.when(step == end + 5)
+    def _():
+        for offset in range(1, prompts):
+            up_piece(lax.rem(prompt + offset, prompts), prompt, offset).wait_recv()
+        for offset in range(1, prompts):
+            up_piece(prompt, lax.rem(prompt + offset, prompts), offset).wait_send()
         rows_all[me] = (low_sum(up_all, prompts) / prompts).astype(LOW)
         rows_start()
 
@@ -478,21 +550,38 @@
         key_down_grad[...] = down[:rank] / prompts
         value_down_grad[...] = down[rank:] / prompts
 
-    @pl.when(step == end + 14)
+    @pl.when(step == end + 12)
     def _():
         rows_finish()
-        key_up_grad[...] = rows_all[: n // 2].astype(jnp.float32).reshape(key_up_grad.shape)
-        value_up_grad[...] = rows_all[n // 2 :].astype(jnp.float32).reshape(value_up_grad.shape)
+        up_whole[prompt] = rows_all[...]
+        whole_start()
+
+    @pl.when(step == end + 18)
+    def _():
+        whole_finish()
+        for owner in range(prompts):
+            columns = slice(owner * portion, (owner + 1) * portion)
+            rows = up_whole[owner].astype(jnp.float32).reshape(2 * rank, portion)
+            key_up_grad[:, columns] = rows[:rank]
+            value_up_grad[:, columns] = rows[rank:]
 
     live, half, index = hide(step - lag)
     for place in range(n):
 
         @pl.when(jnp.logical_and(live, me == place))
         def _():
-            if place < n - 1:
-                high_copy(half, index, up_out, place + 1).wait_send()
-            if place > 0:
-                low_copy(half, index, down_out, place - 1).wait_send()
+            if place == 0:
+                near_up_copy(half, index).wait_send()
+            if place == 1:
+                near_up_copy(half, index).wait_recv()
+            if place == n - 2:
+                near_down_copy(half, index).wait_recv()
+            if place == n - 1:
+                near_down_copy(half, index).wait_send()
+            if place < n - 1 and n > 2:
+                high_copy(half, index, up_out, max(place + 1, 2)).wait_send()
+            if place > 0 and n > 2:
+                low_copy(half, index, down_out, min(place - 1, n - 3)).wait_send()
             own = slice(place * sub, (place + 1) * sub)
             both = (
                 up_in[half, index, :, own].astype(jnp.float32)
@@ -510,6 +599,50 @@
                     grad_text.at[pl.ds(owner * block + side * sub, sub)],
                     text_sem.at[side, owner],
                 ).wait()
+
+
+def store_kernel(count, pieces, *refs):
+    sources, results, stages = refs[:count], refs[count : 2 * count], refs[2 * count : 3 * count]
+    load_sem, store_sem = refs[3 * count :]
+
+    def copies(item, piece):
+        rows = sources[item].shape[0] // pieces[item]
+        at = pl.ds(piece * rows, rows)
+        slot = sum(pieces[:item]) + piece
+        return (
+            pltpu.make_async_copy(
+                sources[item].at[at], stages[item].at[at], load_sem.at[slot]
+            ),
+            pltpu.make_async_copy(
+                stages[item].at[at], results[item].at[at], store_sem.at[slot]
+            ),
+        )
+
+    every = [copies(item, piece) for item in range(count) for piece in range(pieces[item])]
+    for load, _ in every:
+        load.start()
+    for load, store in every:
+        load.wait()
+        store.start()
+    for _, store in every:
+        store.wait()
+
+
+def store(*arrays):
+    pieces = [
+        4 if value.shape[0] % 64 == 0 and value.size >= 2**18 else 1 for value in arrays
+    ]
+    total = sum(pieces)
+    anywhere = pl.BlockSpec(memory_space=pl.ANY)
+    return pl.pallas_call(
+        functools.partial(store_kernel, len(arrays), pieces),
+        out_shape=tuple(jax.ShapeDtypeStruct(value.shape, value.dtype) for value in arrays),
+        in_specs=[anywhere] * len(arrays),
+        out_specs=(anywhere,) * len(arrays),
+        scratch_shapes=[pltpu.VMEM(value.shape, value.dtype) for value in arrays]
+        + [pltpu.SemaphoreType.DMA((total,))] * 2,
+        name="store",
+    )(*arrays)
 
 
 def shards(
@@ -539,7 +672,7 @@
     lag = 2 * (n - 1)
     first = max(2 * heads, heads + lag + 6)
     second = max(first + slices, 2 * heads + lag + 6)
-    steps = max(second + slices + lag, 2 * heads + lag + 14)
+    steps = max(second + slices + lag, 2 * heads + lag + 18)
     block = length // n
     sub = block // 2
     half_length = length // 2
@@ -551,6 +684,7 @@
         heads=heads,
         slices=slices,
         lag=lag,
+        delay=max(0, min(4, lag - 2)),
         first=first,
         second=second,
         steps=steps,
@@ -622,13 +756,15 @@
             pltpu.VMEM((2, splits, half_length, features), LOW),
             pltpu.VMEM((2, splits, half_length, 2 * rank), LOW),
             pltpu.VMEM((2, n, sub, features), LOW),
-            pltpu.VMEM((2, n, 8, half_length), jnp.float32),
+            pltpu.VMEM((2, n, half_length // 128, 128), jnp.float32),
             pltpu.VMEM((n, share, length), LOW),
             pltpu.VMEM((n, share, length), LOW),
             pltpu.VMEM((2, share, half_length), LOW),
             pltpu.VMEM((heads, share, HD), jnp.float32),
-            pltpu.VMEM((prompts, share, columns), LOW),
-            pltpu.VMEM((n, share, columns), LOW),
+            pltpu.VMEM((prompts, share, columns // prompts), LOW),
+            pltpu.VMEM((prompts, share, columns // prompts), LOW),
+            pltpu.VMEM((n, share, columns // prompts), LOW),
+            pltpu.VMEM((prompts, n, share, columns // prompts), LOW),
             pltpu.VMEM((2 * rank, features), jnp.float32),
             pltpu.VMEM((prompts, 2 * rank, features), LOW),
         ]
@@ -639,6 +775,8 @@
         + [dma((n,))] * 2
         + [dma((prompts,))] * 4
         + [dma((n,))] * 2
+        + [dma((prompts,))] * 2
+        + [dma((2, slices))] * 4
         + [dma((2, n))],
         compiler_params=pltpu.CompilerParams(
             collective_id=0, has_side_effects=True, vmem_limit_bytes=62 * 1024 * 1024
@@ -659,6 +797,9 @@
         norm_gain[None, :],
         key_down.T,
         value_down.T,
+    )
+    grad_query, grad_hidden, grad_text, down_key, down_value, up_key, up_value = store(
+        grad_query, grad_hidden, grad_text, down_key, down_value, up_key, up_value
     )
     return (
         grad_query[None],

time: 237 us -> 228 us (0.962)
  local copies, waits for them, and re-layouts: 8.36 us -> 0 us
    unnamed x19 -> x0, local copies, waits for them, and re-layouts: 8.36 us -> none
    pallas_call x1, Pallas kernels: 228 us -> 222 us  [shards(): pl.pallas_call(functools.partial(kernel, plan), grid=(steps,), out_shape=...]
    pallas_call x0 -> x1, Pallas kernels: none -> 5.3 us  [store(): pl.pallas_call(functools.partial(store_kernel, len(arrays), pieces), out_...]
where the time goes in v2:
time: 228 us
  Pallas kernels  227 us (100%)
    pallas_call x1, Pallas kernels, shards(): pl.pallas_call(functools.partial(kernel, plan), grid=(steps,), out_shape=...  222 us
    pallas_call x1, Pallas kernels, store(): pl.pallas_call(functools.partial(store_kernel, len(arrays), pieces), out_...  5.3 us

profile of v2, /device:TPU:0, one launch (start us, length us, event | category | flops | bytes accessed | tf_op | source)
XLA Modules:
  0.0 227.7 jit_solution(1183022463343295880)
XLA Ops:
  0.6 221.8 %fused.1 = (bf16[512,2560]{1,0:T(8,128)(2,1)}, bf16[128,5120]{1,0:T(8,128)(2,1)}, bf16[512,1024]{1,0:T(8,128)(2,1)}, f32[32,1024]{1,0:T(8,128)}, f32[32,1024]{1,...) custom-call(bf16[512,2560]{1,0:T(8,128)(2,1)} %bitcast.13, bf16[512,2560]{1,0:T(8,128)(2,1)} %bitcast.14, ...), custom_call_target="tpu_custom_call" | custom-call | tf_op jit(solution)/shard_map/fused/pallas_call | solution.py:715
  222.4 5.3 %store.1 = (bf16[512,2560]{1,0:T(8,128)(2,1)}, bf16[128,5120]{1,0:T(8,128)(2,1)}, bf16[512,1024]{1,0:T(8,128)(2,1)}, f32[32,1024]{1,0:T(8,128)}, f32[32,1024]{1,...) custom-call(bf16[512,2560]{1,0:T(8,128)(2,1)} %get-tuple-element.21.refs_0_, ...), custom_call_target="tpu_custom_call" | custom-call | tf_op jit(solution)/shard_map/store/pallas_call | solution.py:637

commit v3 on v2

--- a/solution.py
+++ b/solution.py
@@ -102,10 +102,6 @@
     up_recv,
     down_send,
     down_recv,
-    high_send,
-    high_recv,
-    low_send,
-    low_recv,
     context_send,
     context_recv,
     project_send,
@@ -161,12 +157,20 @@
     def column(row, size):
         return jnp.transpose(jnp.broadcast_to(row, (128, size)))[:, :1]
 
+    ring = plan["ring"]
+
+    def heads_ring(half, index):
+        return lax.rem(index + half * heads, ring)
+
+    def hidden_ring(half, index):
+        return lax.rem(first + index + half * (second - first), ring)
+
     def up_copy(half, index, source):
         return pltpu.make_async_remote_copy(
             src_ref=source.at[half, index],
             dst_ref=up_in.at[half, index],
-            send_sem=up_send.at[half, index],
-            recv_sem=up_recv.at[half, index],
+            send_sem=up_send.at[heads_ring(half, index)],
+            recv_sem=up_recv.at[heads_ring(half, index)],
             device_id={"seq": above},
             device_id_type=MESH,
         )
@@ -175,8 +179,8 @@
         return pltpu.make_async_remote_copy(
             src_ref=source.at[half, index],
             dst_ref=down_in.at[half, index],
-            send_sem=down_send.at[half, index],
-            recv_sem=down_recv.at[half, index],
+            send_sem=down_send.at[heads_ring(half, index)],
+            recv_sem=down_recv.at[heads_ring(half, index)],
             device_id={"seq": below},
             device_id_type=MESH,
         )
@@ -186,8 +190,8 @@
         return pltpu.make_async_remote_copy(
             src_ref=source.at[half, index, :, rows],
             dst_ref=up_in.at[half, index, :, rows],
-            send_sem=high_send.at[half, index],
-            recv_sem=high_recv.at[half, index],
+            send_sem=up_send.at[hidden_ring(half, index)],
+            recv_sem=up_recv.at[hidden_ring(half, index)],
             device_id={"seq": above},
             device_id_type=MESH,
         )
@@ -197,8 +201,8 @@
         return pltpu.make_async_remote_copy(
             src_ref=source.at[half, index, :, rows],
             dst_ref=down_in.at[half, index, :, rows],
-            send_sem=low_send.at[half, index],
-            recv_sem=low_recv.at[half, index],
+            send_sem=down_send.at[hidden_ring(half, index)],
+            recv_sem=down_recv.at[hidden_ring(half, index)],
             device_id={"seq": below},
             device_id_type=MESH,
         )
@@ -208,8 +212,8 @@
         return pltpu.make_async_remote_copy(
             src_ref=part.at[half, index, :, rows],
             dst_ref=up_in.at[half, index, :, rows],
-            send_sem=near_up_send.at[half, index],
-            recv_sem=near_up_recv.at[half, index],
+            send_sem=near_up_send.at[hidden_ring(half, index)],
+            recv_sem=near_up_recv.at[hidden_ring(half, index)],
             device_id={"seq": above},
             device_id_type=MESH,
         )
@@ -219,8 +223,8 @@
         return pltpu.make_async_remote_copy(
             src_ref=part.at[half, index, :, rows],
             dst_ref=down_in.at[half, index, :, rows],
-            send_sem=near_down_send.at[half, index],
-            recv_sem=near_down_recv.at[half, index],
+            send_sem=near_down_send.at[hidden_ring(half, index)],
+            recv_sem=near_down_recv.at[hidden_ring(half, index)],
             device_id={"seq": below},
             device_id_type=MESH,
         )
@@ -630,7 +634,7 @@
 
 def store(*arrays):
     pieces = [
-        4 if value.shape[0] % 64 == 0 and value.size >= 2**18 else 1 for value in arrays
+        2 if value.shape[0] % 64 == 0 and value.size >= 2**18 else 1 for value in arrays
     ]
     total = sum(pieces)
     anywhere = pl.BlockSpec(memory_space=pl.ANY)
@@ -684,6 +688,7 @@
         heads=heads,
         slices=slices,
         lag=lag,
+        ring=lag + 4,
         delay=max(0, min(4, lag - 2)),
         first=first,
         second=second,
@@ -768,15 +773,14 @@
             pltpu.VMEM((2 * rank, features), jnp.float32),
             pltpu.VMEM((prompts, 2 * rank, features), LOW),
         ]
-        + [dma((2, heads))] * 4
-        + [dma((2, slices))] * 4
+        + [dma((lag + 4,))] * 4
         + [dma((2, splits))] * 4
         + [dma((2, n))] * 2
         + [dma((n,))] * 2
         + [dma((prompts,))] * 4
         + [dma((n,))] * 2
         + [dma((prompts,))] * 2
-        + [dma((2, slices))] * 4
+        + [dma((lag + 4,))] * 4
         + [dma((2, n))],
         compiler_params=pltpu.CompilerParams(
             collective_id=0, has_side_effects=True, vmem_limit_bytes=62 * 1024 * 1024

time: 228 us -> 224 us (0.982)
  Pallas kernels: 227 us -> 223 us
    pallas_call x1, Pallas kernels: 222 us -> 218 us  [shards(): pl.pallas_call(functools.partial(kernel, plan), grid=(steps,), out_shape=...]
where the time goes in v3:
time: 224 us
  Pallas kernels  223 us (100%)
    pallas_call x1, Pallas kernels, shards(): pl.pallas_call(functools.partial(kernel, plan), grid=(steps,), out_shape=...  218 us
    pallas_call x1, Pallas kernels, store(): pl.pallas_call(functools.partial(store_kernel, len(arrays), pieces), out_...  4.64 us

profile of v3, /device:TPU:0, one launch (start us, length us, event | category | flops | bytes accessed | tf_op | source)
XLA Modules:
  0.0 223.6 jit_solution(2865679959634753142)
XLA Ops:
  0.6 218.3 %fused.1 = (bf16[512,2560]{1,0:T(8,128)(2,1)}, bf16[128,5120]{1,0:T(8,128)(2,1)}, bf16[512,1024]{1,0:T(8,128)(2,1)}, f32[32,1024]{1,0:T(8,128)}, f32[32,1024]{1,...) custom-call(bf16[512,2560]{1,0:T(8,128)(2,1)} %bitcast.13, bf16[512,2560]{1,0:T(8,128)(2,1)} %bitcast.14, ...), custom_call_target="tpu_custom_call" | custom-call | tf_op jit(solution)/shard_map/fused/pallas_call | solution.py:720
  218.9 4.6 %store.1 = (bf16[512,2560]{1,0:T(8,128)(2,1)}, bf16[128,5120]{1,0:T(8,128)(2,1)}, bf16[512,1024]{1,0:T(8,128)(2,1)}, f32[32,1024]{1,0:T(8,128)}, f32[32,1024]{1,...) custom-call(bf16[512,2560]{1,0:T(8,128)(2,1)} %get-tuple-element.21.refs_0_, ...), custom_call_target="tpu_custom_call" | custom-call | tf_op jit(solution)/shard_map/store/pallas_call | solution.py:641

commit v4 on v3

--- a/solution.py
+++ b/solution.py
@@ -285,8 +285,8 @@
         part[half, index, 0] = product[:, :HD]
         part[half, index, 1] = product[:, HD:]
 
-    up_at = step - 2 * me
-    down_at = step - 2 * (n - 1 - me)
+    up_at = step - plan["spacing"] * me
+    down_at = step - plan["spacing"] * (n - 1 - me)
 
     live, half, index = attend(up_at)
 
@@ -673,10 +673,12 @@
     heads = columns // HD
     width = 2 * HD
     slices = hidden // width
-    lag = 2 * (n - 1)
+    spacing = 3
+    lag = spacing * (n - 1)
     first = max(2 * heads, heads + lag + 6)
     second = max(first + slices, 2 * heads + lag + 6)
     steps = max(second + slices + lag, 2 * heads + lag + 18)
+    ring = lag + spacing + 2
     block = length // n
     sub = block // 2
     half_length = length // 2
@@ -688,7 +690,8 @@
         heads=heads,
         slices=slices,
         lag=lag,
-        ring=lag + 4,
+        spacing=spacing,
+        ring=ring,
         delay=max(0, min(4, lag - 2)),
         first=first,
         second=second,
@@ -773,14 +776,14 @@
             pltpu.VMEM((2 * rank, features), jnp.float32),
             pltpu.VMEM((prompts, 2 * rank, features), LOW),
         ]
-        + [dma((lag + 4,))] * 4
+        + [dma((ring,))] * 4
         + [dma((2, splits))] * 4
         + [dma((2, n))] * 2
         + [dma((n,))] * 2
         + [dma((prompts,))] * 4
         + [dma((n,))] * 2
         + [dma((prompts,))] * 2
-        + [dma((lag + 4,))] * 4
+        + [dma((ring,))] * 4
         + [dma((2, n))],
         compiler_params=pltpu.CompilerParams(
             collective_id=0, has_side_effects=True, vmem_limit_bytes=62 * 1024 * 1024

time: 224 us -> 220 us (0.982)
  Pallas kernels: 223 us -> 219 us
    pallas_call x1, Pallas kernels: 218 us -> 215 us  [shards(): pl.pallas_call(functools.partial(kernel, plan), grid=(steps,), out_shape=...]
where the time goes in v4:
time: 220 us
  Pallas kernels  219 us (100%)
    pallas_call x1, Pallas kernels, shards(): pl.pallas_call(functools.partial(kernel, plan), grid=(steps,), out_shape=...  215 us
    pallas_call x1, Pallas kernels, store(): pl.pallas_call(functools.partial(store_kernel, len(arrays), pieces), out_...  4.64 us

profile of v4, /device:TPU:0, one launch (start us, length us, event | category | flops | bytes accessed | tf_op | source)
XLA Modules:
  0.0 220.1 jit_solution(13165143787649860818)
XLA Ops:
  0.6 214.8 %fused.1 = (bf16[512,2560]{1,0:T(8,128)(2,1)}, bf16[128,5120]{1,0:T(8,128)(2,1)}, bf16[512,1024]{1,0:T(8,128)(2,1)}, f32[32,1024]{1,0:T(8,128)}, f32[32,1024]{1,...) custom-call(bf16[512,2560]{1,0:T(8,128)(2,1)} %bitcast.13, bf16[512,2560]{1,0:T(8,128)(2,1)} %bitcast.14, ...), custom_call_target="tpu_custom_call" | custom-call | tf_op jit(solution)/shard_map/fused/pallas_call | solution.py:723
  215.4 4.6 %store.1 = (bf16[512,2560]{1,0:T(8,128)(2,1)}, bf16[128,5120]{1,0:T(8,128)(2,1)}, bf16[512,1024]{1,0:T(8,128)(2,1)}, f32[32,1024]{1,0:T(8,128)}, f32[32,1024]{1,...) custom-call(bf16[512,2560]{1,0:T(8,128)(2,1)} %get-tuple-element.21.refs_0_, ...), custom_call_target="tpu_custom_call" | custom-call | tf_op jit(solution)/shard_map/store/pallas_call | solution.py:641

commit v5 on v4

--- a/solution.py
+++ b/solution.py
@@ -65,7 +65,7 @@
     key_up,
     value_up,
     out_weight,
-    normed,
+    normed_whole,
     scale,
     gain,
     key_down,
@@ -123,6 +123,8 @@
     near_down_send,
     near_down_recv,
     text_sem,
+    normed,
+    normed_sem,
 ):
     n, splits, prompts = plan["n"], plan["splits"], plan["prompts"]
     heads, slices, lag = plan["heads"], plan["slices"], plan["lag"]
@@ -245,14 +247,15 @@
     @pl.when(step == 0)
     def _():
         barrier = pltpu.get_barrier_semaphore()
-        for axis, size in (("tp", splits), ("seq", n), ("dp", prompts)):
-            for offset in range(1, size):
+        for axis, size in (("seq", n), ("dp", prompts), ("tp", splits)):
+            for offset in reversed(range(1, size)):
                 pl.semaphore_signal(
                     barrier,
                     inc=1,
                     device_id={axis: lax.rem(lax.axis_index(axis) + offset, size)},
                     device_id_type=MESH,
                 )
+        pltpu.make_async_copy(normed_whole, normed, normed_sem).start()
 
     @pl.when(step < heads)
     def _():
@@ -390,6 +393,7 @@
 
     @pl.when(step == 1)
     def _():
+        pltpu.make_async_copy(normed_whole, normed, normed_sem).wait()
         down = jnp.concatenate([key_down[...], value_down[...]], axis=0)
         sides = [dot(down, context_of(side), 1, 1) for side in range(2)]
         latent_own[...] = (
@@ -633,9 +637,7 @@
 
 
 def store(*arrays):
-    pieces = [
-        2 if value.shape[0] % 64 == 0 and value.size >= 2**18 else 1 for value in arrays
-    ]
+    pieces = [1] * len(arrays)
     total = sum(pieces)
     anywhere = pl.BlockSpec(memory_space=pl.ANY)
     return pl.pallas_call(
@@ -742,7 +744,7 @@
             late(rank),
             late(rank),
             pl.BlockSpec((width, features), lambda step: (slice_of(step)[1], 0)),
-            fixed(length, features),
+            pl.BlockSpec(memory_space=pl.ANY),
             fixed(1, length),
             fixed(1, features),
             fixed(rank, features),
@@ -784,7 +786,8 @@
         + [dma((n,))] * 2
         + [dma((prompts,))] * 2
         + [dma((ring,))] * 4
-        + [dma((2, n))],
+        + [dma((2, n))]
+        + [pltpu.VMEM((length, features), LOW), dma],
         compiler_params=pltpu.CompilerParams(
             collective_id=0, has_side_effects=True, vmem_limit_bytes=62 * 1024 * 1024
         ),

time: 220 us -> 219 us (level)
  no operation moved by 1% of the time
where the time goes in v5:
time: 219 us
  Pallas kernels  219 us (100%)
    pallas_call x1, Pallas kernels, shards(): pl.pallas_call(functools.partial(kernel, plan), grid=(steps,), out_shape=...  214 us
    pallas_call x1, Pallas kernels, store(): pl.pallas_call(functools.partial(store_kernel, len(arrays), pieces), out_...  4.4 us

profile of v5, /device:TPU:0, one launch (start us, length us, event | category | flops | bytes accessed | tf_op | source)
XLA Modules:
  0.0 219.2 jit_solution(3392574312249825573)
XLA Ops:
  0.6 214.1 %fused.1 = (bf16[512,2560]{1,0:T(8,128)(2,1)}, bf16[128,5120]{1,0:T(8,128)(2,1)}, bf16[512,1024]{1,0:T(8,128)(2,1)}, f32[32,1024]{1,0:T(8,128)}, f32[32,1024]{1,...) custom-call(bf16[512,2560]{1,0:T(8,128)(2,1)} %bitcast.13, bf16[512,2560]{1,0:T(8,128)(2,1)} %bitcast.14, ...), custom_call_target="tpu_custom_call" | custom-call | tf_op jit(solution)/shard_map/fused/pallas_call | solution.py:725
  214.8 4.4 %store.1 = (bf16[512,2560]{1,0:T(8,128)(2,1)}, bf16[128,5120]{1,0:T(8,128)(2,1)}, bf16[512,1024]{1,0:T(8,128)(2,1)}, f32[32,1024]{1,0:T(8,128)}, f32[32,1024]{1,...) custom-call(bf16[512,2560]{1,0:T(8,128)(2,1)} %get-tuple-element.21.refs_0_, ...), custom_call_target="tpu_custom_call" | custom-call | tf_op jit(solution)/shard_map/store/pallas_call | solution.py:643

commit v6 on v5

--- a/solution.py
+++ b/solution.py
@@ -260,8 +260,8 @@
     @pl.when(step < heads)
     def _():
         query, key, value, grad = queries[...], keys[...], values[...], grads[...]
-        scores = dot(key, query, 1, 1) * factor
-        weights = jnp.exp(scores - jnp.max(scores, axis=0, keepdims=True))
+        scores = dot(key, query, 1, 1)
+        weights = jnp.exp((scores - jnp.max(scores, axis=0, keepdims=True)) * factor)
         probability = weights * (1.0 / jnp.sum(weights, axis=0, keepdims=True))
         value_part = dot(probability.astype(LOW), grad, 1, 0).astype(LOW)
         grad_probs = dot(value, grad, 1, 1)

time: 219 us -> 219 us (level)
  no operation moved by 1% of the time
where the time goes in v6:
time: 219 us
  Pallas kernels  219 us (100%)
    pallas_call x1, Pallas kernels, shards(): pl.pallas_call(functools.partial(kernel, plan), grid=(steps,), out_shape=...  214 us
    pallas_call x1, Pallas kernels, store(): pl.pallas_call(functools.partial(store_kernel, len(arrays), pieces), out_...  4.4 us

profile of v6, /device:TPU:0, one launch (start us, length us, event | category | flops | bytes accessed | tf_op | source)
XLA Modules:
  0.0 219.2 jit_solution(9922875671535729432)
XLA Ops:
  0.6 214.1 %fused.1 = (bf16[512,2560]{1,0:T(8,128)(2,1)}, bf16[128,5120]{1,0:T(8,128)(2,1)}, bf16[512,1024]{1,0:T(8,128)(2,1)}, f32[32,1024]{1,0:T(8,128)}, f32[32,1024]{1,...) custom-call(bf16[512,2560]{1,0:T(8,128)(2,1)} %bitcast.13, bf16[512,2560]{1,0:T(8,128)(2,1)} %bitcast.14, ...), custom_call_target="tpu_custom_call" | custom-call | tf_op jit(solution)/shard_map/fused/pallas_call | solution.py:725
  214.7 4.4 %store.1 = (bf16[512,2560]{1,0:T(8,128)(2,1)}, bf16[128,5120]{1,0:T(8,128)(2,1)}, bf16[512,1024]{1,0:T(8,128)(2,1)}, f32[32,1024]{1,0:T(8,128)}, f32[32,1024]{1,...) custom-call(bf16[512,2560]{1,0:T(8,128)(2,1)} %get-tuple-element.21.refs_0_, ...), custom_call_target="tpu_custom_call" | custom-call | tf_op jit(solution)/shard_map/store/pallas_call | solution.py:643
